TPU v7x, 32 devices: a whole 2x2x4 slice. The times are simulated.
32 devices in a mesh: row: 4 (over y, x), col: 8 (over z, core).
Axes of the slice: x: 2, y: 2, z: 4, core: 2. Of those that a mesh axis runs over, the one named last changes fastest.
Arguments:
- stiffness: float32 [12, 4, 128, 6144], P(None, 'row', None, 'col'), may hold values from -8 to 8
- lower_first: float32 [1024, 10, 4, 128], P('col', None, 'row'), may hold values from -0.1875 to 0.1875
- lower_second: float32 [1024, 8, 4, 128], P('col', None, 'row'), may hold values from -0.1875 to 0.1875
- diag_inv: float32 [2, 1024, 2, 4, 128], P(None, 'col', None, 'row'), as said below
Outputs:
- reduced: float32 [12, 4, 128, 6144], P(None, 'row', None, 'col')
Inputs may be any that keep to these rules, and one draw needn't show every extreme that they name: Each block of diag_inv, read as a 1024 x 1024 matrix, is zero above its diagonal and has a positive diagonal.
All inputs are finite; a program needn't handle non-finite values.
Results may differ from a plain program's by a relative error of at most 0.000086.
Values sent between devices are 32-bit elements; how exact they have to be, the bound alone decides.
A program may use at most 128 MiB of HBM per device.

v0:
```python
import jax
import jax.numpy as jnp
from jax import lax
from jax.sharding import PartitionSpec as P


def product(left, right):
    return jnp.dot(left, right, precision=lax.Precision.HIGH, preferred_element_type=jnp.float32)


def apply_cols(columns, factor):
    return lax.dot_general(
        columns,
        factor,
        (((0,), (0,)), ((), ())),
        precision=lax.Precision.HIGH,
        preferred_element_type=jnp.float32,
    )


def shards(stiffness, lower_first, lower_second, diag_inv):
    cycles = stiffness.shape[0]
    rblk = stiffness.shape[2]
    cdev = stiffness.shape[3]
    pcount = diag_inv.shape[2]
    nrow = lax.axis_size("row")
    nb = diag_inv.shape[1] * lax.axis_size("col")
    height = pcount * rblk
    matrix_rows = stiffness.reshape(cycles * rblk, cdev)
    inv_cols = lax.all_gather(diag_inv, "col", axis=1, tiled=True)
    inverse = inv_cols.reshape(2, nb, height)

    def own_rows(solved):
        grouped = solved.reshape(pcount, nrow, rblk, cdev)
        mine = lax.dynamic_slice_in_dim(grouped, lax.axis_index("row"), 1, 1)
        return mine.reshape(height, cdev)

    w_first = lax.psum(product(inverse[0], matrix_rows[:height]), "row")
    coupling = lax.all_gather(lower_first[:, :pcount], "col", axis=0, tiled=True).reshape(
        nb, height
    )
    w_second = lax.psum(
        product(inverse[1], matrix_rows[height : 2 * height] - apply_cols(coupling, w_first)), "row"
    )
    pieces = (
        lax.all_gather(lower_first[:, pcount:], "col", axis=0, tiled=True),
        lax.all_gather(lower_second, "col", axis=0, tiled=True),
    )
    count = pieces[0].shape[0]
    first_piece = pieces[0].reshape(count, -1)
    second_piece = pieces[1].reshape(count, -1)
    remain = (
        matrix_rows[2 * height :]
        - apply_cols(first_piece, w_first)
        - apply_cols(second_piece, w_second)
    )
    stacked = jnp.concatenate([own_rows(w_first), own_rows(w_second), remain], axis=0)
    return stacked.reshape(cycles, 1, rblk, cdev)


def solution(mesh):
    placed = (
        P(None, "row", None, "col"),
        P("col", None, "row", None),
        P("col", None, "row", None),
        P(None, "col", None, "row", None),
    )
    return jax.shard_map(
        shards, mesh=mesh, in_specs=placed, out_specs=P(None, "row", None, "col"), check_vma=False
    )
```

profile of v0, /device:TPU:0, one launch (start us, length us, event | category | flops | bytes accessed | tf_op | source)
XLA Modules:
  0.0 369.2 jit_solution(9611690720741950493)
XLA Ops:
  6.5 0.0 all-gather.5.cloned.1.call-start
  6.5 0.7 all-gather.5.cloned.1.call-update
  7.3 0.0 all-gather.7.cloned.1.call-start
  7.3 1.6 slice.37
  8.9 0.0 all-gather.7.cloned.1.call-update
  8.9 0.0 all-reduce.3.cloned.1.call-start
  8.9 1.5 fusion.16
  10.4 30.4 %all-gather.5.cloned.1.call-done = f32[2,1024,2,1,128]{4,3,2,1,0:T(1,128)} async-done(((f32[2,128,2,1,128]{4,3,2,1,0:T(1,128)}), f32[2,1024,2,1,128]{4,3,2,1,0:T(1,128)}) %all-gather.5.cloned.1.call-update) | async-done | bytes 2097168 | tf_op jit(solution)/shard_map/all_gather | solution.py:30
  40.8 7.8 %slice_reduce_fusion = (f32[1024,2,128]{2,1,0:T(2,128)S(1)}, f32[1024,2,128]{2,1,0:T(2,128)S(1)}) fusion(f32[2,1024,2,1,128]{4,3,2,1,0:T(1,128)} %all-gather.5.cloned.1.call-done), kind=kLoop, calls=%fused_computation.19 | loop fusion | bytes 4194304 | tf_op jit(solution)/shard_map/slice | solution.py:43
  48.7 3.1 fusion.13
  51.8 0.0 all-reduce.3.cloned.1.call-update
  51.8 0.0 all-reduce.5.cloned.1.call-start
  51.9 0.3 copy.21
  52.2 12.0 %all-gather.7.cloned.1.call-done = f32[1024,2,1,128]{3,1,2,0:T(2,128)} async-done(((f32[128,2,1,128]{3,1,2,0:T(2,128)}), f32[1024,2,1,128]{3,1,2,0:T(2,128)}) %all-gather.7.cloned.1.call-update) | async-done | bytes 1048592 | tf_op jit(solution)/shard_map/all_gather | solution.py:39
  64.1 89.7 %all-reduce.3.cloned.1.call-done = f32[1024,768]{1,0:T(8,128)} async-done(((f32[1024,768]{1,0:T(8,128)}), f32[1024,768]{1,0:T(8,128)}) %all-reduce.3.cloned.1.call-update) | async-done | bytes 3145744 | tf_op jit(solution)/shard_map/psum | solution.py:38
  153.8 4.8 %fusion.8 = f32[256,768]{0,1:T(8,128)S(1)} fusion(f32[256,768]{0,1:T(8,128)S(1)} %copy.21, f32[1024,768]{1,0:T(8,128)} %all-reduce.3.cloned.1.call-done, f32[128,8,2,128]{3,2,1,0:T(2,128)} %bitcast.76), kind=kOutput, calls=%fused_computation.11 | convolution fusion | flops 1208156160 | bytes 5767168 | tf_op jit(solution)/shard_map/dot_general | solution.py:12
  158.6 0.0 copy-start.3
  158.6 3.1 convolution_bitcast_fusion
  161.7 0.0 all-reduce.5.cloned.1.call-update
  161.7 0.0 all-gather.11.cloned.1.call-start
  161.8 0.5 all-gather.11.cloned.1.call-update
  162.3 0.2 all-gather.9.cloned.1.call-start
  162.5 0.0 copy-done.3
  162.6 0.8 slice.41
  163.4 0.0 all-gather.9.cloned.1.call-update
  163.4 3.8 %slice.39 = f32[8,1,128,768]{3,2,1,0:T(8,128)} slice(f32[12,1,128,768]{3,2,1,0:T(8,128)} %param.4), slice={[4:12], [0:1], [0:128], [0:768]} | slice | bytes 6291456 | tf_op jit(solution)/shard_map/slice | solution.py:53
  167.2 0.0 copy-start
  167.2 4.1 %copy.22 = f32[1024,768]{0,1:T(8,128)} copy(f32[1024,768]{1,0:T(8,128)} %bitcast.65) | data formatting | bytes 6291456 | tf_op jit(solution)/shard_map/slice | solution.py:53
  171.3 0.0 copy-done
  171.3 0.9 constant_dynamic-slice_fusion
  172.3 2.3 copy.20
  174.6 74.3 %all-reduce.5.cloned.1.call-done = f32[1024,768]{0,1:T(8,128)} async-done(((f32[1024,768]{0,1:T(8,128)}), f32[1024,768]{0,1:T(8,128)}) %all-reduce.5.cloned.1.call-update) | async-done | bytes 3145744 | tf_op jit(solution)/shard_map/psum | solution.py:42
  248.8 5.1 %reshape.36 = f32[2,4,128,768]{2,1,0,3:T(4,128)} reshape(f32[1024,768]{0,1:T(8,128)} %all-reduce.5.cloned.1.call-done) | data formatting | bytes 6291456 | tf_op jit(solution)/shard_map/reshape | solution.py:34
  254.0 4.6 %dynamic-slice_reduce_fusion = f32[2,128,768]{1,0,2:T(2,128)S(1)} fusion(f32[2,4,128,768]{2,1,0,3:T(4,128)} %reshape.36, s32[]{:T(128)S(6)} %select_n.4), kind=kLoop, calls=%fused_computation.22 | loop fusion | bytes 1572868 | tf_op jit(solution)/shard_map/dynamic_slice | solution.py:35
  258.5 0.9 copy.54
  259.5 37.7 %all-gather.11.cloned.1.call-done = f32[1024,8,1,128]{3,1,2,0:T(8,128)} async-done(((f32[128,8,1,128]{3,1,2,0:T(8,128)}), f32[1024,8,1,128]{3,1,2,0:T(8,128)}) %all-gather.11.cloned.1.call-update) | async-done | bytes 4194320 | tf_op jit(solution)/shard_map/all_gather | solution.py:47
  297.2 9.6 %fusion = f32[768,1024]{1,0:T(8,128)} fusion(f32[1024,768]{0,1:T(8,128)} %all-reduce.5.cloned.1.call-done, f32[128,8,8,128]{3,2,1,0:T(8,128)} %bitcast.66), kind=kOutput, calls=%fused_computation.1 | convolution fusion | flops 4831838208 | bytes 10485760 | tf_op jit(solution)/shard_map/dot_general | solution.py:12
  306.8 37.6 %all-gather.9.cloned.1.call-done = f32[1024,8,1,128]{3,1,2,0:T(8,128)} async-done(((f32[128,8,1,128]{3,1,2,0:T(8,128)}), f32[1024,8,1,128]{3,1,2,0:T(8,128)}) %all-gather.9.cloned.1.call-update) | async-done | bytes 4194320 | tf_op jit(solution)/shard_map/all_gather | solution.py:46
  344.3 0.0 copy-start.1
  344.3 0.0 copy-start.2
  344.3 9.4 %bitcast_subtract_fusion = f32[1024,768]{0,1:T(8,128)S(1)} fusion(f32[768,1024]{1,0:T(8,128)} %fusion, f32[1024,768]{0,1:T(8,128)} %copy.22, f32[1024,768]{1,0:T(8,128)S(1)} %copy-done, f32[128,8,8,128]{3,2,1,0:T(8,128)} %bitcast.69), kind=kOutput, calls=%fused_computation.7 | convolution fusion | flops 4833411072 | bytes 16777216 | tf_op jit(solution)/shard_map/dot_general | solution.py:12
  353.7 0.0 copy-done.1
  353.8 0.0 copy-done.2
  353.8 2.6 pad_maximum_fusion
  356.4 6.0 %copy.18 = f32[1536,768]{1,0:T(8,128)} copy(f32[1536,768]{0,1:T(8,128)} %pad_maximum_fusion) | data formatting | bytes 9437184 | tf_op jit(solution)/shard_map/concatenate | solution.py:57
Async XLA Ops:
  6.5 34.3 %all-gather.5.cloned.1.call-start = ((), (), s32[]{:S(2)}) async-start(), calls=%async_computation | async-start | bytes 2359296 | tf_op jit(solution)/shard_map/all_gather | solution.py:30
  7.3 56.9 %all-gather.7.cloned.1.call-start = ((), (), s32[]{:S(2)}) async-start(), calls=%async_computation.2 | async-start | bytes 1179648 | tf_op jit(solution)/shard_map/all_gather | solution.py:39
  8.9 144.9 %all-reduce.3.cloned.1.call-start = ((), (), s32[]{:S(2)}) async-start(), calls=%async_computation.1 | async-start | bytes 6291456 | tf_op jit(solution)/shard_map/psum | solution.py:38
  51.8 197.0 %all-reduce.5.cloned.1.call-start = ((), (), s32[]{:S(2)}) async-start(), calls=%async_computation.3 | async-start | bytes 6291456 | tf_op jit(solution)/shard_map/psum | solution.py:42
  158.6 4.0 %copy-start.3 = (f32[128,10,1,128]{3,2,1,0:T(1,128)S(1)}, f32[128,10,1,128]{3,2,1,0:T(1,128)}, u32[]{:S(2)}) copy-start(f32[128,10,1,128]{3,2,1,0:T(1,128)} %param.5) | copy-start | bytes 1966084
  161.7 135.4 %all-gather.11.cloned.1.call-start = ((), (), s32[]{:S(2)}) async-start(), calls=%async_computation.5 | async-start | bytes 4718592 | tf_op jit(solution)/shard_map/all_gather | solution.py:47
  162.3 182.0 %all-gather.9.cloned.1.call-start = ((), (), s32[]{:S(2)}) async-start(), calls=%async_computation.4 | async-start | bytes 4718592 | tf_op jit(solution)/shard_map/all_gather | solution.py:46
  167.2 4.1 %copy-start = (f32[1024,768]{1,0:T(8,128)S(1)}, f32[1024,768]{1,0:T(8,128)}, u32[]{:S(2)}) copy-start(f32[1024,768]{1,0:T(8,128)} %all-reduce.3.cloned.1.call-done) | copy-start | bytes 9437188
  344.3 9.4 %copy-start.1 = (f32[256,768]{0,1:T(8,128)S(1)}, f32[256,768]{0,1:T(8,128)}, u32[]{:S(2)}) copy-start(f32[256,768]{0,1:T(8,128)} %copy.20) | copy-start | bytes 2359300
  344.3 9.4 %copy-start.2 = (f32[96,8,2,128]{3,1,2,0:T(8,128)S(1)}, f32[96,8,2,128]{3,1,2,0:T(8,128)}, u32[]{:S(2)}) copy-start(f32[96,8,2,128]{3,1,2,0:T(8,128)} %copy.54) | copy-start | bytes 2359300
Sparse Core Ops, SparseCore 0:
  8.9 31.8 all-gather.4
  42.4 21.6 all-gather.6
  67.2 86.5 all-reduce.2
  161.9 86.9 all-reduce.4
  250.3 46.8 all-gather.10
  298.6 45.6 all-gather.8
where the time goes:
time: 370 us; the launch traced here: 369 us
  waiting for transfers between devices  283 us (76%)
  local copies, waits for them, and re-layouts  39.8 us (11%)
  matrix products  30 us (8%)
  between operations  13.6 us (4%)
    psum x1, waiting for transfers between devices, shards(): w_first = lax.psum(product(inverse[0], matrix_rows[:height]), 'row')  89.7 us
    psum x1, waiting for transfers between devices, shards(): lax.psum(product(inverse[1], matrix_rows[height:2 * height] - apply_cols(...  74.3 us
    all_gather x1, waiting for transfers between devices, shards(): lax.all_gather(lower_second, 'col', axis=0, tiled=True)  37.7 us
    all_gather x1, waiting for transfers between devices, shards(): lax.all_gather(lower_first[:, pcount:], 'col', axis=0, tiled=True)  37.6 us
    all_gather x1, waiting for transfers between devices, shards(): inv_cols = lax.all_gather(diag_inv, 'col', axis=1, tiled=True)  30.4 us
    dot_general x3, matrix products, apply_cols(): lax.dot_general(columns, factor, (((0,), (0,)), ((), ())), precision=lax....  23.8 us
    all_gather x1, waiting for transfers between devices, shards(): lax.all_gather(lower_first[:, :pcount], 'col', axis=0, tiled=True)  12 us
    slice x2, local copies, waits for them, and re-layouts, shards(): matrix_rows[2 * height:] - apply_cols(first_piece, w_first)  7.89 us
  transfers between devices with their start and end apart: 6, of which 6 were waited for; matrix products, arithmetic and copies ran while one was open for 13% of the time, Pallas kernels for 0%

commit v1 on v0

--- a/solution.py
+++ b/solution.py
@@ -39,8 +39,12 @@
     coupling = lax.all_gather(lower_first[:, :pcount], "col", axis=0, tiled=True).reshape(
         nb, height
     )
-    w_second = lax.psum(
-        product(inverse[1], matrix_rows[height : 2 * height] - apply_cols(coupling, w_first)), "row"
+    w_second = jnp.sum(
+        lax.all_gather(
+            product(inverse[1], matrix_rows[height : 2 * height] - apply_cols(coupling, w_first)),
+            "row",
+        ),
+        axis=0,
     )
     pieces = (
         lax.all_gather(lower_first[:, pcount:], "col", axis=0, tiled=True),

time: 370 us -> 406 us (1.097)
  waiting for transfers between devices: 283 us -> 301 us
  other arithmetic: 2.59 us -> 12.5 us
  local copies, waits for them, and re-layouts: 39.8 us -> 47.3 us
    all_gather x0 -> x1, waiting for transfers between devices: none -> 114 us  [shards(): lax.all_gather(product(inverse[1], matrix_rows[height:2 * height] - apply...]
    psum x1 -> x0, waiting for transfers between devices: 74.3 us -> none  [shards(): lax.psum(product(inverse[1], matrix_rows[height:2 * height] - apply_cols(...]
    all_gather x1, waiting for transfers between devices: 37.7 us -> 15.9 us  [shards(): lax.all_gather(lower_second, 'col', axis=0, tiled=True)]
    all_gather x0 -> x1, local copies, waits for them, and re-layouts: none -> 15.7 us  [shards(): lax.all_gather(product(inverse[1], matrix_rows[height:2 * height] - apply...]
    reduce_sum x0 -> x1, other arithmetic: none -> 9.95 us  [shards(): jnp.sum(lax.all_gather(product(inverse[1], matrix_rows[height:2 * height]...]
    reshape x1 -> x0, local copies, waits for them, and re-layouts: 5.13 us -> none  [own_rows(): grouped = solved.reshape(pcount, nrow, rblk, cdev)]
  transfers between devices with their start and end apart: 6 -> 6, of which waited for: 6 -> 6; matrix products, arithmetic and copies ran while one was open for 13% -> 15% of each run, Pallas kernels for 0% -> 0%
where the time goes in v1:
time: 406 us
  waiting for transfers between devices  301 us (74%)
  local copies, waits for them, and re-layouts  47.3 us (12%)
  matrix products  30.4 us (7%)
  between operations  13.6 us (3%)
  other arithmetic  12.5 us (3%)
    all_gather x1, waiting for transfers between devices, shards(): lax.all_gather(product(inverse[1], matrix_rows[height:2 * height] - apply...  114 us
    psum x1, waiting for transfers between devices, shards(): w_first = lax.psum(product(inverse[0], matrix_rows[:height]), 'row')  89.7 us
    all_gather x1, waiting for transfers between devices, shards(): lax.all_gather(lower_first[:, pcount:], 'col', axis=0, tiled=True)  38.1 us
    all_gather x1, waiting for transfers between devices, shards(): inv_cols = lax.all_gather(diag_inv, 'col', axis=1, tiled=True)  30.4 us
    dot_general x3, matrix products, apply_cols(): lax.dot_general(columns, factor, (((0,), (0,)), ((), ())), precision=lax....  24.1 us
    all_gather x1, waiting for transfers between devices, shards(): lax.all_gather(lower_second, 'col', axis=0, tiled=True)  15.9 us
    all_gather x1, local copies, waits for them, and re-layouts, shards(): lax.all_gather(product(inverse[1], matrix_rows[height:2 * height] - apply...  15.7 us
    all_gather x1, waiting for transfers between devices, shards(): lax.all_gather(lower_first[:, :pcount], 'col', axis=0, tiled=True)  12 us
  transfers between devices with their start and end apart: 6, of which 6 were waited for; matrix products, arithmetic and copies ran while one was open for 15% of the time, Pallas kernels for 0%

profile of v1, /device:TPU:0, one launch (start us, length us, event | category | flops | bytes accessed | tf_op | source)
XLA Modules:
  0.0 405.6 jit_solution(12816044676412542944)
XLA Ops:
  6.5 0.0 all-gather.7.cloned.1.call-start
  6.5 0.7 all-gather.7.cloned.1.call-update
  7.3 0.0 all-gather.9.cloned.1.call-start
  7.3 1.6 slice.37
  8.9 0.0 all-gather.9.cloned.1.call-update
  8.9 0.0 all-reduce.2.cloned.1.call-start
  8.9 1.5 fusion.16
  10.4 30.4 %all-gather.7.cloned.1.call-done = f32[2,1024,2,1,128]{4,3,2,1,0:T(1,128)} async-done(((f32[2,128,2,1,128]{4,3,2,1,0:T(1,128)}), f32[2,1024,2,1,128]{4,3,2,1,0:T(1,128)}) %all-gather.7.cloned.1.call-update) | async-done | bytes 2097168 | tf_op jit(solution)/shard_map/all_gather | solution.py:30
  40.8 7.8 %slice_reduce_fusion = (f32[1024,2,128]{2,1,0:T(2,128)S(1)}, f32[1024,2,128]{2,1,0:T(2,128)S(1)}) fusion(f32[2,1024,2,1,128]{4,3,2,1,0:T(1,128)} %all-gather.7.cloned.1.call-done), kind=kLoop, calls=%fused_computation.19 | loop fusion | bytes 4194304 | tf_op jit(solution)/shard_map/slice | solution.py:44
  48.7 3.1 fusion.13
  51.8 0.0 all-reduce.2.cloned.1.call-update
  51.8 0.0 all-gather.15.cloned.1.call-start
  51.9 0.3 copy.24
  52.2 12.0 %all-gather.9.cloned.1.call-done = f32[1024,2,1,128]{3,1,2,0:T(2,128)} async-done(((f32[128,2,1,128]{3,1,2,0:T(2,128)}), f32[1024,2,1,128]{3,1,2,0:T(2,128)}) %all-gather.9.cloned.1.call-update) | async-done | bytes 1048592 | tf_op jit(solution)/shard_map/all_gather | solution.py:39
  64.1 89.7 %all-reduce.2.cloned.1.call-done = f32[1024,768]{1,0:T(8,128)} async-done(((f32[1024,768]{1,0:T(8,128)}), f32[1024,768]{1,0:T(8,128)}) %all-reduce.2.cloned.1.call-update) | async-done | bytes 3145744 | tf_op jit(solution)/shard_map/psum | solution.py:38
  153.8 4.8 %fusion.8 = f32[256,768]{0,1:T(8,128)S(1)} fusion(f32[256,768]{0,1:T(8,128)S(1)} %copy.24, f32[1024,768]{1,0:T(8,128)} %all-reduce.2.cloned.1.call-done, f32[128,8,2,128]{3,2,1,0:T(2,128)} %bitcast.72), kind=kOutput, calls=%fused_computation.11 | convolution fusion | flops 1208156160 | bytes 5767168 | tf_op jit(solution)/shard_map/dot_general | solution.py:12
  158.6 0.0 copy-start.2
  158.6 3.1 convolution_bitcast_fusion
  161.7 0.0 all-gather.15.cloned.1.call-update
  161.7 0.0 all-gather.13.cloned.1.call-start
  161.8 0.5 all-gather.13.cloned.1.call-update
  162.3 0.2 all-gather.11.cloned.1.call-start
  162.5 0.0 copy-done.2
  162.6 0.8 slice.41
  163.4 0.0 all-gather.11.cloned.1.call-update
  163.4 0.0 slice-start
  163.4 1.9 slice-done
  165.3 2.3 copy.26
  167.6 1.3 constant_dynamic-slice_fusion.1
  169.0 1.2 copy.23
  170.2 114.1 %all-gather.15.cloned.1.call-done = f32[4096,768]{0,1:T(8,128)} async-done(((f32[1024,768]{0,1:T(8,128)}), f32[4096,768]{0,1:T(8,128)}) %all-gather.15.cloned.1.call-update) | async-done | bytes 12582928 | tf_op jit(solution)/shard_map/all_gather | solution.py:43
  284.3 15.7 %reshape.41 = f32[4,1024,768]{1,0,2:T(4,128)} reshape(f32[4096,768]{0,1:T(8,128)} %all-gather.15.cloned.1.call-done) | data formatting | bytes 25165824 | tf_op jit(solution)/shard_map/all_gather | solution.py:43
  300.0 9.9 %reduce_sum.9 = f32[1024,768]{0,1:T(8,128)S(1)} reduce(f32[4,1024,768]{1,0,2:T(4,128)} %reshape.41, f32[]{:T(128)} %constant.10.clone.1), dimensions={0}, to_apply=%region_1.0 | reduce | flops 2359296 | bytes 15728644 | tf_op jit(solution)/shard_map/reduce_sum | solution.py:42
  309.9 2.4 copy.16
  312.3 2.1 constant_dynamic-slice_fusion
  314.4 2.3 copy.25
  316.7 15.9 %all-gather.13.cloned.1.call-done = f32[1024,8,1,128]{3,1,2,0:T(8,128)} async-done(((f32[128,8,1,128]{3,1,2,0:T(8,128)}), f32[1024,8,1,128]{3,1,2,0:T(8,128)}) %all-gather.13.cloned.1.call-update) | async-done | bytes 4194320 | tf_op jit(solution)/shard_map/all_gather | solution.py:51
  332.6 9.1 %fusion = f32[768,1024]{1,0:T(8,128)} fusion(f32[1024,768]{0,1:T(8,128)S(1)} %reduce_sum.9, f32[128,8,8,128]{3,2,1,0:T(8,128)} %bitcast.63), kind=kOutput, calls=%fused_computation.1 | convolution fusion | flops 4831838208 | bytes 10485760 | tf_op jit(solution)/shard_map/dot_general | solution.py:12
  341.7 38.1 %all-gather.11.cloned.1.call-done = f32[1024,8,1,128]{3,1,2,0:T(8,128)} async-done(((f32[128,8,1,128]{3,1,2,0:T(8,128)}), f32[1024,8,1,128]{3,1,2,0:T(8,128)}) %all-gather.11.cloned.1.call-update) | async-done | bytes 4194320 | tf_op jit(solution)/shard_map/all_gather | solution.py:50
  379.8 0.0 copy-start
  379.8 0.0 copy-start.1
  379.8 10.3 %bitcast_subtract_fusion = f32[1024,768]{0,1:T(8,128)S(1)} fusion(f32[768,1024]{1,0:T(8,128)} %fusion, f32[1024,768]{0,1:T(8,128)} %copy.26, f32[1024,768]{1,0:T(8,128)} %all-reduce.2.cloned.1.call-done, f32[128,8,8,128]{3,2,1,0:T(8,128)} %bitcast.66), kind=kOutput, calls=%fused_computation.7 | convolution fusion | flops 4833411072 | bytes 16777216 | tf_op jit(solution)/shard_map/dot_general | solution.py:12
  390.1 0.0 copy-done
  390.1 0.0 copy-done.1
  390.1 2.6 pad_maximum_fusion
  392.7 6.0 %copy.21 = f32[1536,768]{1,0:T(8,128)} copy(f32[1536,768]{0,1:T(8,128)} %pad_maximum_fusion) | data formatting | bytes 9437184 | tf_op jit(solution)/shard_map/concatenate | solution.py:61
Async XLA Ops:
  6.5 34.3 %all-gather.7.cloned.1.call-start = ((), (), s32[]{:S(2)}) async-start(), calls=%async_computation | async-start | bytes 2359296 | tf_op jit(solution)/shard_map/all_gather | solution.py:30
  7.3 56.9 %all-gather.9.cloned.1.call-start = ((), (), s32[]{:S(2)}) async-start(), calls=%async_computation.2 | async-start | bytes 1179648 | tf_op jit(solution)/shard_map/all_gather | solution.py:39
  8.9 144.9 %all-reduce.2.cloned.1.call-start = ((), (), s32[]{:S(2)}) async-start(), calls=%async_computation.1 | async-start | bytes 6291456 | tf_op jit(solution)/shard_map/psum | solution.py:38
  51.8 232.4 %all-gather.15.cloned.1.call-start = ((), (), s32[]{:S(2)}) async-start(), calls=%async_computation.5 | async-start | bytes 15728640 | tf_op jit(solution)/shard_map/all_gather | solution.py:43
  158.6 4.0 copy-start.2
  161.7 170.9 %all-gather.13.cloned.1.call-start = ((), (), s32[]{:S(2)}) async-start(), calls=%async_computation.4 | async-start | bytes 4718592 | tf_op jit(solution)/shard_map/all_gather | solution.py:51
  162.3 217.5 %all-gather.11.cloned.1.call-start = ((), (), s32[]{:S(2)}) async-start(), calls=%async_computation.3 | async-start | bytes 4718592 | tf_op jit(solution)/shard_map/all_gather | solution.py:50
  163.4 1.9 slice-start
  379.8 10.3 %copy-start = (f32[256,768]{0,1:T(8,128)S(1)}, f32[256,768]{0,1:T(8,128)}, u32[]{:S(2)}) copy-start(f32[256,768]{0,1:T(8,128)} %copy.23) | copy-start | bytes 2359300
  379.8 10.3 %copy-start.1 = (f32[256,768]{0,1:T(8,128)S(1)}, f32[256,768]{0,1:T(8,128)}, u32[]{:S(2)}) copy-start(f32[256,768]{0,1:T(8,128)} %copy.25) | copy-start | bytes 2359300
Sparse Core Ops, SparseCore 0:
  8.9 31.8 all-gather.6
  42.4 21.6 all-gather.8
  67.2 86.5 all-reduce.1
  161.9 122.3 all-gather.14
  285.7 46.8 all-gather.12
  334.1 45.6 all-gather.10
